TPU v7x, 32 devices: a whole 2x2x4 slice. The times are simulated.
32 devices in a mesh: rep: 8 (over z, x), exp: 4 (over y, core).
Axes of the slice: x: 2, y: 2, z: 4, core: 2. Of those that a mesh axis runs over, the one named last changes fastest.
Arguments:
- expert_ids: int32 [8, 512, 8], P('rep', 'exp'), may hold values from 0 to 15, as said below
- route_weights: bfloat16 [8, 512, 8], P('rep', 'exp'), may hold values from 0.049804688 to 0.59765625
- out_grad: bfloat16 [8, 512, 1024], P('rep', 'exp'), may hold values from -6 to 6
- saved_inputs: bfloat16 [8, 4, 32, 1024], P('rep', 'exp'), may hold values from -6 to 6
- gate_weight: bfloat16 [4, 1024, 384], P('exp', 'rep'), may hold values from -0.1875 to 0.1875
- up_weight: bfloat16 [4, 1024, 384], P('exp', 'rep'), may hold values from -0.1875 to 0.1875
- down_weight: bfloat16 [4, 1024, 384], P('exp', 'rep'), may hold values from -0.3125 to 0.3125
Outputs:
- input_grad: bfloat16 [8, 512, 1024], P('rep', 'exp')
- route_grad: bfloat16 [8, 512, 8], P('rep', 'exp')
- gate_grad: float32 [4, 1024, 384], P('exp', 'rep')
- up_grad: float32 [4, 1024, 384], P('exp', 'rep')
- down_grad: float32 [4, 1024, 384], P('exp', 'rep')
Inputs may be any that keep to these rules, and one draw needn't show every extreme that they name: `expert_ids`: each row names 8 different experts. Within each aligned block of 128 rows of one replica, an expert e with e % 4 == 0 is named at most 8 times; for every replica, some such expert is named exactly 8 times in each of its blocks.
All inputs are finite; a program needn't handle non-finite values.
Results may differ from a plain program's by a relative error of at most 0.014.
Values may be sent and summed in bfloat16 or wider, within the bound.
No kernel may reach another device: no remote copies, remote signals or barrier semaphores. Data moves between devices by JAX's collectives and lax.ppermute only.
A program may use at most 64 MiB of HBM per device.

v0:
```python
import jax
import jax.numpy as jnp
from jax import lax
from jax.sharding import PartitionSpec as P

TOPK = 8
EXP_DEV = 4


def slot_table(block_ids, slot_count, owners):
    flat_ids = block_ids.reshape(-1)
    chosen = flat_ids % EXP_DEV == 0
    owner_of = flat_ids // EXP_DEV
    capacity = slot_count // owners
    onehot = ((owner_of[:, None] == jnp.arange(owners)[None, :]) & chosen[:, None]).astype(
        jnp.int32
    )
    earlier = jnp.cumsum(onehot, axis=0) - onehot
    position = jnp.sum(earlier * onehot, axis=1)
    slot_of = jnp.where(chosen, owner_of * capacity + position, -1)
    return slot_of[None, :] == jnp.arange(slot_count)[:, None]


def first_contract(left, right):
    return lax.dot_general(
        left, right, (((0,), (0,)), ((), ())), preferred_element_type=jnp.float32
    )


def second_contract(left, right):
    return lax.dot_general(
        left, right, (((1,), (1,)), ((), ())), preferred_element_type=jnp.float32
    )


def body(expert_ids, route_weights, out_grad, saved_inputs, gate_weight, up_weight, down_weight):
    owners = lax.axis_size("exp")
    replicas = lax.axis_size("rep")
    tokens_here = out_grad.shape[1]
    features = out_grad.shape[2]
    hidden_width = gate_weight.shape[2]
    slot_count = saved_inputs.shape[2]
    capacity = slot_count // owners
    placed = slot_table(expert_ids[0], slot_count, owners)
    weights_flat = route_weights[0].reshape(-1)
    slot_scale = jnp.sum(
        jnp.where(placed, weights_flat[None, :], jnp.zeros((), weights_flat.dtype)), axis=1
    )
    token_hits = jnp.any(placed.reshape(slot_count, tokens_here, TOPK), axis=2)
    token_of = jnp.sum(jnp.where(token_hits, jnp.arange(tokens_here)[None, :], 0), axis=1)
    is_live = jnp.any(token_hits, axis=1)
    routed = jnp.where(is_live[:, None], out_grad[0][token_of], jnp.zeros((), jnp.bfloat16))
    arrived, arrived_scale = (
        lax.all_to_all(
            routed.reshape(owners, capacity, features),
            "exp",
            split_axis=0,
            concat_axis=0,
            tiled=True,
        ),
        lax.all_to_all(
            slot_scale.reshape(owners, capacity), "exp", split_axis=0, concat_axis=0, tiled=True
        ),
    )
    full_gate, full_up, full_down = (
        lax.all_gather(gate_weight[0], "rep", axis=0, tiled=True),
        lax.all_gather(up_weight[0], "rep", axis=0, tiled=True),
        lax.all_gather(down_weight[0], "rep", axis=0, tiled=True),
    )
    grad_rows = arrived.reshape(slot_count, features)
    scale_col = arrived_scale.reshape(slot_count, 1).astype(jnp.float32)
    inputs_here = saved_inputs[0, 0]
    pre_gate = jnp.dot(inputs_here, full_gate, preferred_element_type=jnp.float32)
    pre_up = jnp.dot(inputs_here, full_up, preferred_element_type=jnp.float32)
    sigmoid_gate = jax.nn.sigmoid(pre_gate)
    activated = pre_gate * sigmoid_gate
    hidden = (activated * pre_up).astype(jnp.bfloat16)
    raw_grad = jnp.dot(grad_rows, full_down, preferred_element_type=jnp.float32)
    slot_route = jnp.sum(hidden.astype(jnp.float32) * raw_grad, axis=1).astype(jnp.bfloat16)
    hidden_grad = scale_col * raw_grad
    scaled_rows = (scale_col * grad_rows.astype(jnp.float32)).astype(jnp.bfloat16)
    gate_delta = (
        hidden_grad * pre_up * sigmoid_gate * (1.0 + pre_gate * (1.0 - sigmoid_gate))
    ).astype(jnp.bfloat16)
    up_delta = (hidden_grad * activated).astype(jnp.bfloat16)
    back_rows = (
        second_contract(gate_delta, full_gate) + second_contract(up_delta, full_up)
    ).astype(jnp.bfloat16)
    returned, returned_route = (
        lax.all_to_all(
            back_rows.reshape(owners, capacity, features),
            "exp",
            split_axis=0,
            concat_axis=0,
            tiled=True,
        ),
        lax.all_to_all(
            slot_route.reshape(owners, capacity), "exp", split_axis=0, concat_axis=0, tiled=True
        ),
    )
    returned_flat = returned.reshape(slot_count, features)
    route_flat = returned_route.reshape(slot_count)
    combined = jax.ops.segment_sum(
        jnp.where(is_live[:, None], returned_flat.astype(jnp.float32), 0.0),
        token_of,
        num_segments=tokens_here,
    )
    input_grad = combined.astype(jnp.bfloat16)[None]
    route_grad = jnp.sum(
        jnp.where(placed, route_flat[:, None], jnp.zeros((), jnp.bfloat16)), axis=0
    )
    route_grad = route_grad.reshape(1, tokens_here, TOPK)
    joined_share = lax.psum_scatter(
        jnp.concatenate(
            [
                jnp.concatenate(
                    [
                        first_contract(inputs_here, gate_delta),
                        first_contract(inputs_here, up_delta),
                    ],
                    axis=1,
                ),
                first_contract(scaled_rows, hidden),
            ],
            axis=1,
        ),
        "rep",
        scatter_dimension=0,
        tiled=True,
    )
    gate_share = joined_share[:, :hidden_width]
    up_share = joined_share[:, hidden_width : 2 * hidden_width]
    down_share = joined_share[:, 2 * hidden_width :]
    gate_grad = (gate_share / replicas)[None]
    up_grad = (up_share / replicas)[None]
    down_grad = (down_share / replicas)[None]
    return (input_grad, route_grad, gate_grad, up_grad, down_grad)


def solution(mesh):
    in_specs = (
        P("rep", "exp", None),
        P("rep", "exp", None),
        P("rep", "exp", None),
        P("rep", "exp", None, None),
        P("exp", "rep", None),
        P("exp", "rep", None),
        P("exp", "rep", None),
    )
    out_specs = (
        P("rep", "exp", None),
        P("rep", "exp", None),
        P("exp", "rep", None),
        P("exp", "rep", None),
        P("exp", "rep", None),
    )
    return jax.shard_map(body, mesh=mesh, in_specs=in_specs, out_specs=out_specs, check_vma=False)
```

profile of v0, /device:TPU:0, one launch (start us, length us, event | category | flops | bytes accessed | tf_op | source)
XLA Modules:
  0.0 239.1 jit_solution(11610807980264724344)
XLA Ops:
  7.2 0.8 copy.44
  8.3 1.1 reduce-window.6
  10.2 0.7 fusion.18
  11.1 0.6 gather_fusion
  11.7 0.7 bitcast_select_fusion
  12.4 4.2 %all-to-all-start.1 = ((bf16[4,8,1024]{2,1,0:T(8,128)(2,1)}), bf16[4,8,1024]{2,1,0:T(8,128)(2,1)S(1)}, u32[]{:S(2)}, u32[]{:S(2)}) async-start(bf16[4,8,1024]{2,1,0:T(8,128)(2,1)} %bitcast_select_fusion), calls=%async_computation.1 | async-start | bytes 131072 | tf_op jit(solution)/shard_map/all_to_all | solution.py:54
  16.7 33.0 %all-gather.2 = bf16[1,1024,384]{2,1,0:T(8,128)(2,1)S(1)} all-gather(bf16[1,128,384]{2,1,0:T(8,128)(2,1)S(1)} %copy-done.2), channel_id=4, replica_groups=mesh['rep'=8,'exp'=4] {'rep'}, dimensions={1}, use_global_device_ids=true | all-gather | bytes 884736 | tf_op jit(solution)/shard_map/all_gather | solution.py:66
  49.7 32.4 %all-gather.1 = bf16[1,1024,384]{2,1,0:T(8,128)(2,1)S(1)} all-gather(bf16[1,128,384]{2,1,0:T(8,128)(2,1)S(1)} %copy-done.3), channel_id=3, replica_groups=mesh['rep'=8,'exp'=4] {'rep'}, dimensions={1}, use_global_device_ids=true | all-gather | bytes 884736 | tf_op jit(solution)/shard_map/all_gather | solution.py:67
  82.6 32.0 %all-gather = bf16[1,1024,384]{2,1,0:T(8,128)(2,1)S(1)} all-gather(bf16[1,128,384]{2,1,0:T(8,128)(2,1)S(1)} %copy-done.4), channel_id=2, replica_groups=mesh['rep'=8,'exp'=4] {'rep'}, dimensions={1}, use_global_device_ids=true | all-gather | bytes 884736 | tf_op jit(solution)/shard_map/all_gather | solution.py:68
  115.2 7.2 %all_to_all.26 = bf16[4,1,8]{2,1,0:T(2,128)(2,1)S(1)} all-to-all(bf16[4,1,8]{2,1,0:T(2,128)(2,1)S(1)} %convert_element_type.84), channel_id=1, replica_groups=mesh['rep'=8,'exp'=4] {'exp'}, dimensions={0} | all-to-all | bytes 128 | tf_op jit(solution)/shard_map/all_to_all | solution.py:97
  122.7 6.1 %all_to_all.27 = bf16[4,1,8]{2,1,0:T(2,128)(2,1)S(1)} all-to-all(bf16[4,1,8]{2,1,0:T(2,128)(2,1)S(1)} %all_to_all.21), channel_id=1, replica_groups=mesh['rep'=8,'exp'=4] {'exp'}, dimensions={0} | all-to-all | bytes 128 | tf_op jit(solution)/shard_map/all_to_all | solution.py:61
  129.8 0.4 fusion.26
  130.2 2.5 %pad_maximum_fusion = f32[1024,1152]{0,1:T(8,128)} fusion(f32[1024,384]{0,1:T(8,128)S(1)} %fusion.26, f32[1024,384]{0,1:T(8,128)S(1)} %convolution_bitcast_fusion, f32[1024,384]{0,1:T(8,128)S(1)} %convolution_bitcast_fusion.1), kind=kLoop, calls=%fused_computation.2 | loop fusion | flops 2359296 | bytes 9437184 | tf_op jit(solution)/shard_map/concatenate | solution.py:114
  133.1 1.0 fusion.1
  134.1 3.3 %all-to-all-start.2 = ((bf16[4,8,1024]{2,1,0:T(8,128)(2,1)}), bf16[4,8,1024]{2,1,0:T(8,128)(2,1)S(1)}, u32[]{:S(2)}, u32[]{:S(2)}) async-start(bf16[4,8,1024]{2,1,0:T(8,128)(2,1)} %fusion.1), calls=%async_computation.2 | async-start | bytes 131072 | tf_op jit(solution)/shard_map/all_to_all | solution.py:90
  137.5 0.7 copy.51
  138.1 3.3 %all-to-all-done.2 = bf16[4,8,1024]{2,1,0:T(8,128)(2,1)S(1)} async-done(((bf16[4,8,1024]{2,1,0:T(8,128)(2,1)}), bf16[4,8,1024]{2,1,0:T(8,128)(2,1)S(1)}, u32[]{:S(2)}, u32[]{:S(2)}) %all-to-all-start.2) | async-done | bytes 65568 | tf_op jit(solution)/shard_map/all_to_all | solution.py:90
  141.5 1.0 scatter_custom_fusion
  142.5 0.7 convert_bitcast_fusion
  143.3 85.4 %reduce-scatter.2.cloned.1.call-done = f32[128,1152]{0,1:T(8,128)} async-done(((f32[1024,1152]{0,1:T(8,128)}), f32[128,1152]{0,1:T(8,128)}) %reduce-scatter.2.cloned.1.call-update) | async-done | bytes 589840 | tf_op jit(solution)/shard_map/reduce_scatter | solution.py:113
  228.6 1.2 fusion.13
  229.8 0.8 copy.54
  230.6 0.8 copy.53
  231.4 0.8 copy.52
  (51 shorter events, 4.0 us)
Async XLA Ops:
  7.2 3.9 %copy-start = (bf16[1,128,1024]{2,1,0:T(8,128)(2,1)S(1)}, bf16[1,128,1024]{2,1,0:T(8,128)(2,1)}, u32[]{:S(2)}) copy-start(bf16[1,128,1024]{2,1,0:T(8,128)(2,1)} %param.9) | copy-start | bytes 786436
  7.2 9.5 %copy-start.2 = (bf16[1,128,384]{2,1,0:T(8,128)(2,1)S(1)}, bf16[1,128,384]{2,1,0:T(8,128)(2,1)}, u32[]{:S(2)}) copy-start(bf16[1,128,384]{2,1,0:T(8,128)(2,1)} %param.11) | copy-start | bytes 294916
  7.2 42.5 %copy-start.3 = (bf16[1,128,384]{2,1,0:T(8,128)(2,1)S(1)}, bf16[1,128,384]{2,1,0:T(8,128)(2,1)}, u32[]{:S(2)}) copy-start(bf16[1,128,384]{2,1,0:T(8,128)(2,1)} %param.12) | copy-start | bytes 294916
  8.2 73.9 %copy-start.1 = (bf16[1,1,32,1024]{3,2,1,0:T(8,128)(2,1)S(1)}, bf16[1,1,32,1024]{3,2,1,0:T(8,128)(2,1)}, u32[]{:S(2)}) copy-start(bf16[1,1,32,1024]{3,2,1,0:T(8,128)(2,1)} %param.10) | copy-start | bytes 196612
  12.4 102.4 %all-to-all-start.1 = ((bf16[4,8,1024]{2,1,0:T(8,128)(2,1)}), bf16[4,8,1024]{2,1,0:T(8,128)(2,1)S(1)}, u32[]{:S(2)}, u32[]{:S(2)}) async-start(bf16[4,8,1024]{2,1,0:T(8,128)(2,1)} %bitcast_select_fusion), calls=%async_computation.1 | async-start | bytes 131072 | tf_op jit(solution)/shard_map/all_to_all | solution.py:54
  16.7 65.9 %copy-start.4 = (bf16[1,128,384]{2,1,0:T(8,128)(2,1)S(1)}, bf16[1,128,384]{2,1,0:T(8,128)(2,1)}, u32[]{:S(2)}) copy-start(bf16[1,128,384]{2,1,0:T(8,128)(2,1)} %param.13) | copy-start | bytes 294916
  16.7 211.9 %reduce-scatter.2.cloned.1.call-start = ((), (), s32[]{:S(2)}) async-start(), calls=%async_computation.5 | async-start | bytes 5308416 | tf_op jit(solution)/shard_map/reduce_scatter | solution.py:113
  49.7 64.8 %copy-start.5 = (bf16[1,128,8]{1,2,0:T(8,128)(2,1)S(1)}, bf16[1,128,8]{1,2,0:T(8,128)(2,1)}, u32[]{:S(2)}) copy-start(bf16[1,128,8]{1,2,0:T(8,128)(2,1)} %param.8) | copy-start | bytes 6148
  134.1 7.4 %all-to-all-start.2 = ((bf16[4,8,1024]{2,1,0:T(8,128)(2,1)}), bf16[4,8,1024]{2,1,0:T(8,128)(2,1)S(1)}, u32[]{:S(2)}, u32[]{:S(2)}) async-start(bf16[4,8,1024]{2,1,0:T(8,128)(2,1)} %fusion.1), calls=%async_computation.2 | async-start | bytes 131072 | tf_op jit(solution)/shard_map/all_to_all | solution.py:90
Sparse Core Ops, SparseCore 0:
  132.9 95.7 reduce-scatter.1
where the time goes:
time: 240 us; the launch traced here: 239 us
  blocking collectives  111 us (46%)
  waiting for transfers between devices  88.7 us (37%)
  between operations  14.2 us (6%)
  other arithmetic  8.79 us (4%)
  starting transfers between devices  7.52 us (3%)
  local copies, waits for them, and re-layouts  5.86 us (2%)
  matrix products  3.3 us (1%)
    reduce_scatter x1, waiting for transfers between devices, body(): lax.psum_scatter(jnp.concatenate([jnp.concatenate([first_contract(inputs_...  85.4 us
    all_gather x1, blocking collectives, body(): lax.all_gather(gate_weight[0], 'rep', axis=0, tiled=True)  33 us
    all_gather x1, blocking collectives, body(): lax.all_gather(up_weight[0], 'rep', axis=0, tiled=True)  32.4 us
    all_gather x1, blocking collectives, body(): lax.all_gather(down_weight[0], 'rep', axis=0, tiled=True)  32 us
    all_to_all x1, blocking collectives, body(): lax.all_to_all(slot_route.reshape(owners, capacity), 'exp', split_axis=0,...  7.19 us
    all_to_all x1, blocking collectives, body(): lax.all_to_all(slot_scale.reshape(owners, capacity), 'exp', split_axis=0,...  6.08 us
  transfers between devices with their start and end apart: 3, of which 2 were waited for; matrix products, arithmetic and copies ran while one was open for 2% of the time, Pallas kernels for 0%

commit v1 on v0

--- a/solution.py
+++ b/solution.py
@@ -5,6 +5,22 @@
 
 TOPK = 8
 EXP_DEV = 4
+
+
+def pairwise_exchange(x, axis, split, join):
+    ways, here = (lax.axis_size(axis), lax.axis_index(axis))
+    width = x.shape[split] // ways
+    lengths = list(x.shape)
+    lengths[split] = width
+    height = lengths[join]
+    lengths[join] = height * ways
+    full = jnp.zeros(lengths, x.dtype)
+    for mask in range(ways):
+        part = lax.dynamic_slice_in_dim(x, (here ^ mask) * width, width, axis=split)
+        if mask:
+            part = lax.ppermute(part, axis, [(d, d ^ mask) for d in range(ways)])
+        full = lax.dynamic_update_slice_in_dim(full, part, (here ^ mask) * height, axis=join)
+    return full
 
 
 def slot_table(block_ids, slot_count, owners):
@@ -87,13 +103,7 @@
         second_contract(gate_delta, full_gate) + second_contract(up_delta, full_up)
     ).astype(jnp.bfloat16)
     returned, returned_route = (
-        lax.all_to_all(
-            back_rows.reshape(owners, capacity, features),
-            "exp",
-            split_axis=0,
-            concat_axis=0,
-            tiled=True,
-        ),
+        pairwise_exchange(back_rows.reshape(owners, capacity, features), "exp", 0, 0),
         lax.all_to_all(
             slot_route.reshape(owners, capacity), "exp", split_axis=0, concat_axis=0, tiled=True
         ),

time: 240 us -> 239 us (level)
    all_to_all x1 -> x0, waiting for transfers between devices: 3.33 us -> none  [body(): lax.all_to_all(back_rows.reshape(owners, capacity, features), 'exp', spli...]
    all_to_all x1 -> x0, starting transfers between devices: 3.28 us -> none  [body(): lax.all_to_all(back_rows.reshape(owners, capacity, features), 'exp', spli...]
    reduce_scatter x1, waiting for transfers between devices: 85.4 us -> 88.5 us  [body(): lax.psum_scatter(jnp.concatenate([jnp.concatenate([first_contract(inputs_...]
  transfers between devices with their start and end apart: 3 -> 5, of which waited for: 2 -> 2; matrix products, arithmetic and copies ran while one was open for 2% -> 2% of each run, Pallas kernels for 0% -> 0%
where the time goes in v1:
time: 239 us
  blocking collectives  111 us (46%)
  waiting for transfers between devices  90.4 us (38%)
  between operations  14.3 us (6%)
  other arithmetic  8.79 us (4%)
  starting transfers between devices  6.44 us (3%)
  local copies, waits for them, and re-layouts  5.9 us (2%)
  matrix products  2.66 us (1%)
    reduce_scatter x1, waiting for transfers between devices, body(): lax.psum_scatter(jnp.concatenate([jnp.concatenate([first_contract(inputs_...  88.5 us
    all_gather x1, blocking collectives, body(): lax.all_gather(gate_weight[0], 'rep', axis=0, tiled=True)  33 us
    all_gather x1, blocking collectives, body(): lax.all_gather(up_weight[0], 'rep', axis=0, tiled=True)  32.4 us
    all_gather x1, blocking collectives, body(): lax.all_gather(down_weight[0], 'rep', axis=0, tiled=True)  32 us
    all_to_all x1, blocking collectives, body(): lax.all_to_all(slot_route.reshape(owners, capacity), 'exp', split_axis=0,...  7.19 us
    all_to_all x1, blocking collectives, body(): lax.all_to_all(slot_scale.reshape(owners, capacity), 'exp', split_axis=0,...  6.08 us
  transfers between devices with their start and end apart: 5, of which 2 were waited for; matrix products, arithmetic and copies ran while one was open for 2% of the time, Pallas kernels for 0%

profile of v1, /device:TPU:0, one launch (start us, length us, event | category | flops | bytes accessed | tf_op | source)
XLA Modules:
  0.0 239.1 jit_solution(14823011745648414814)
XLA Ops:
  7.2 0.8 copy.44
  8.3 1.1 reduce-window.6
  10.2 0.7 fusion.18
  11.1 0.6 gather_fusion
  11.7 0.7 bitcast_select_fusion
  12.4 4.2 %all-to-all-start.1 = ((bf16[4,8,1024]{2,1,0:T(8,128)(2,1)}), bf16[4,8,1024]{2,1,0:T(8,128)(2,1)S(1)}, u32[]{:S(2)}, u32[]{:S(2)}) async-start(bf16[4,8,1024]{2,1,0:T(8,128)(2,1)} %bitcast_select_fusion), calls=%async_computation.1 | async-start | bytes 131072 | tf_op jit(solution)/shard_map/all_to_all | solution.py:70
  16.7 33.0 %all-gather.2 = bf16[1,1024,384]{2,1,0:T(8,128)(2,1)S(1)} all-gather(bf16[1,128,384]{2,1,0:T(8,128)(2,1)S(1)} %copy-done.2), channel_id=4, replica_groups=mesh['rep'=8,'exp'=4] {'rep'}, dimensions={1}, use_global_device_ids=true | all-gather | bytes 884736 | tf_op jit(solution)/shard_map/all_gather | solution.py:82
  49.7 32.4 %all-gather.1 = bf16[1,1024,384]{2,1,0:T(8,128)(2,1)S(1)} all-gather(bf16[1,128,384]{2,1,0:T(8,128)(2,1)S(1)} %copy-done.3), channel_id=3, replica_groups=mesh['rep'=8,'exp'=4] {'rep'}, dimensions={1}, use_global_device_ids=true | all-gather | bytes 884736 | tf_op jit(solution)/shard_map/all_gather | solution.py:83
  82.6 32.0 %all-gather = bf16[1,1024,384]{2,1,0:T(8,128)(2,1)S(1)} all-gather(bf16[1,128,384]{2,1,0:T(8,128)(2,1)S(1)} %copy-done.4), channel_id=2, replica_groups=mesh['rep'=8,'exp'=4] {'rep'}, dimensions={1}, use_global_device_ids=true | all-gather | bytes 884736 | tf_op jit(solution)/shard_map/all_gather | solution.py:84
  115.2 7.2 %all_to_all.21 = bf16[4,1,8]{2,1,0:T(2,128)(2,1)S(1)} all-to-all(bf16[4,1,8]{2,1,0:T(2,128)(2,1)S(1)} %convert_element_type.84), channel_id=1, replica_groups=mesh['rep'=8,'exp'=4] {'exp'}, dimensions={0} | all-to-all | bytes 128 | tf_op jit(solution)/shard_map/all_to_all | solution.py:107
  122.7 6.1 %all_to_all.22 = bf16[4,1,8]{2,1,0:T(2,128)(2,1)S(1)} all-to-all(bf16[4,1,8]{2,1,0:T(2,128)(2,1)S(1)} %all_to_all.17), channel_id=1, replica_groups=mesh['rep'=8,'exp'=4] {'exp'}, dimensions={0} | all-to-all | bytes 128 | tf_op jit(solution)/shard_map/all_to_all | solution.py:77
  129.0 0.4 convolution_bitcast_fusion
  129.8 0.4 fusion.26
  130.2 2.5 %pad_maximum_fusion = f32[1024,1152]{0,1:T(8,128)} fusion(f32[1024,384]{0,1:T(8,128)S(1)} %fusion.26, f32[1024,384]{0,1:T(8,128)S(1)} %convolution_bitcast_fusion, f32[1024,384]{0,1:T(8,128)S(1)} %convolution_bitcast_fusion.1), kind=kLoop, calls=%fused_computation.2 | loop fusion | flops 2359296 | bytes 9437184 | tf_op jit(solution)/shard_map/concatenate | solution.py:124
  133.7 0.7 copy.51
  134.5 2.0 collective-permute-start.1
  136.5 1.9 collective-permute-done.1
  138.4 1.0 scatter_custom_fusion
  139.4 0.7 convert_bitcast_fusion
  140.2 88.5 %reduce-scatter.2.cloned.1.call-done = f32[128,1152]{0,1:T(8,128)} async-done(((f32[1024,1152]{0,1:T(8,128)}), f32[128,1152]{0,1:T(8,128)}) %reduce-scatter.2.cloned.1.call-update) | async-done | bytes 589840 | tf_op jit(solution)/shard_map/reduce_scatter | solution.py:123
  228.6 1.2 fusion.13
  229.8 0.8 copy.54
  230.6 0.8 copy.53
  231.4 0.8 copy.52
  (60 shorter events, 4.2 us)
Async XLA Ops:
  7.2 3.9 %copy-start = (bf16[1,128,1024]{2,1,0:T(8,128)(2,1)S(1)}, bf16[1,128,1024]{2,1,0:T(8,128)(2,1)}, u32[]{:S(2)}) copy-start(bf16[1,128,1024]{2,1,0:T(8,128)(2,1)} %param.9) | copy-start | bytes 786436
  7.2 9.5 %copy-start.2 = (bf16[1,128,384]{2,1,0:T(8,128)(2,1)S(1)}, bf16[1,128,384]{2,1,0:T(8,128)(2,1)}, u32[]{:S(2)}) copy-start(bf16[1,128,384]{2,1,0:T(8,128)(2,1)} %param.11) | copy-start | bytes 294916
  7.2 42.5 %copy-start.3 = (bf16[1,128,384]{2,1,0:T(8,128)(2,1)S(1)}, bf16[1,128,384]{2,1,0:T(8,128)(2,1)}, u32[]{:S(2)}) copy-start(bf16[1,128,384]{2,1,0:T(8,128)(2,1)} %param.12) | copy-start | bytes 294916
  8.2 73.9 %copy-start.1 = (bf16[1,1,32,1024]{3,2,1,0:T(8,128)(2,1)S(1)}, bf16[1,1,32,1024]{3,2,1,0:T(8,128)(2,1)}, u32[]{:S(2)}) copy-start(bf16[1,1,32,1024]{3,2,1,0:T(8,128)(2,1)} %param.10) | copy-start | bytes 196612
  12.4 102.4 %all-to-all-start.1 = ((bf16[4,8,1024]{2,1,0:T(8,128)(2,1)}), bf16[4,8,1024]{2,1,0:T(8,128)(2,1)S(1)}, u32[]{:S(2)}, u32[]{:S(2)}) async-start(bf16[4,8,1024]{2,1,0:T(8,128)(2,1)} %bitcast_select_fusion), calls=%async_computation.1 | async-start | bytes 131072 | tf_op jit(solution)/shard_map/all_to_all | solution.py:70
  16.7 65.9 %copy-start.4 = (bf16[1,128,384]{2,1,0:T(8,128)(2,1)S(1)}, bf16[1,128,384]{2,1,0:T(8,128)(2,1)}, u32[]{:S(2)}) copy-start(bf16[1,128,384]{2,1,0:T(8,128)(2,1)} %param.13) | copy-start | bytes 294916
  16.7 211.9 %reduce-scatter.2.cloned.1.call-start = ((), (), s32[]{:S(2)}) async-start(), calls=%async_computation.4 | async-start | bytes 5308416 | tf_op jit(solution)/shard_map/reduce_scatter | solution.py:123
  49.7 64.8 %copy-start.5 = (bf16[1,128,8]{1,2,0:T(8,128)(2,1)S(1)}, bf16[1,128,8]{1,2,0:T(8,128)(2,1)}, u32[]{:S(2)}) copy-start(bf16[1,128,8]{1,2,0:T(8,128)(2,1)} %param.8) | copy-start | bytes 6148
  133.5 3.0 %collective-permute-start = (bf16[1,8,1024]{2,1,0:T(8,128)(2,1)S(1)}, bf16[1,8,1024]{2,1,0:T(8,128)(2,1)S(1)}, u32[]{:S(2)}, u32[]{:S(2)}) collective-permute-start(bf16[1,8,1024]{2,1,0:T(8,128)(2,1)S(1)} %get-tuple-element.43), channel_id=1, source_target_pairs={{0,1},{1,0},{2,3},{3,2},{4,5},{5,4},{6,7},{7,6},{8,9},{9,8},{10,11... | collective-permute-start | bytes 49160 | tf_op jit(solution)/shard_map/ppermute | solution.py:21
  134.3 4.0 %collective-permute-start.2 = (bf16[1,8,1024]{2,1,0:T(8,128)(2,1)S(1)}, bf16[1,8,1024]{2,1,0:T(8,128)(2,1)S(1)}, u32[]{:S(2)}, u32[]{:S(2)}) collective-permute-start(bf16[1,8,1024]{2,1,0:T(8,128)(2,1)S(1)} %get-tuple-element.41), channel_id=1, source_target_pairs={{0,3},{1,2},{2,1},{3,0},{4,7},{5,6},{6,5},{7,4},{8,11},{9,10},{10,... | collective-permute-start | bytes 49160 | tf_op jit(solution)/shard_map/ppermute | solution.py:21
  134.5 3.9 %collective-permute-start.1 = (bf16[1,8,1024]{2,1,0:T(8,128)(2,1)S(1)}, bf16[1,8,1024]{2,1,0:T(8,128)(2,1)S(1)}, u32[]{:S(2)}, u32[]{:S(2)}) collective-permute-start(bf16[1,8,1024]{2,1,0:T(8,128)(2,1)S(1)} %get-tuple-element.42), channel_id=1, source_target_pairs={{0,2},{1,3},{2,0},{3,1},{4,6},{5,7},{6,4},{7,5},{8,10},{9,11},{10,... | collective-permute-start | bytes 49160 | tf_op jit(solution)/shard_map/ppermute | solution.py:21
Sparse Core Ops, SparseCore 0:
  132.9 95.7 reduce-scatter.1
